TPU v7x, 32 devices: a whole 2x2x4 slice. The times are simulated.
32 devices in a mesh: group: 2 (over x), cell: 16 (over z, y, core).
Axes of the slice: x: 2, y: 2, z: 4, core: 2. Of those that a mesh axis runs over, the one named last changes fastest.
Arguments:
- scen_inputs: float32 [384, 4], P('cell'), may hold values from -1 to 1
- yields: bfloat16 [384, 10, 64, 256], P('cell', None, None, 'group'), parts along dimension 3, may hold values from -6 to 6
- crop_mask: int32 [64, 256], P('cell', 'group'), parts along dimension 1, may hold values 0 or 1
Outputs:
- coefs: float32 [64, 34, 256], P('cell', None, 'group'), parts along dimension 2
- residual: float32 [64, 34, 256], P('cell', None, 'group'), parts along dimension 2
There are 2 independent parts, one for each index of `group`. A program takes and returns all parts, laid end to end along the dimension named above; an argument that names none is the same for every part. Nothing has to cross between parts.
All inputs are finite; a program needn't handle non-finite values. No bound on the sum of `crop_mask` on one device may be relied on, other than what follows from the above.
Results may differ from a plain program's by a relative error of at most 0.0026.
Values sent between devices are 32-bit elements; how exact they have to be, the bound alone decides.
A program may use at most 64 MiB of HBM per device.

v0:
```python
import jax
import jax.numpy as jnp
from jax import lax
from jax.sharding import PartitionSpec as P

ITERS = 3


lambda_smooth = 0.5
ridge_term = 0.05


def padded_2(block, sides, width):
    for axis, dim in sides:
        count = lax.axis_size(axis)
        forward = [(i, i + 1) for i in range(count - 1)]
        backward = [(target, source) for source, target in forward]
        low = lax.ppermute(
            lax.slice_in_dim(block, block.shape[dim] - width, None, axis=dim), axis, forward
        )
        high = lax.ppermute(lax.slice_in_dim(block, 0, width, axis=dim), axis, backward)
        block = jnp.concatenate([low, block, high], axis=dim)
    return block


def design_terms(levels):
    parts = [levels[:, 0], levels[:, 1], levels[:, 2], levels[:, 3]]
    columns = [jnp.ones_like(parts[0])] + parts + [a * a for a in parts]
    for i in range(4):
        for j in range(i + 1, 4):
            columns.append(parts[i] * parts[j])
    columns = columns + [a * a * a for a in parts]
    for i in range(4):
        for j in range(4):
            if i != j:
                columns.append(parts[i] * parts[i] * parts[j])
    carbon, temper, water, nitro = parts
    columns = columns + [carbon * temper * water, carbon * temper * nitro, carbon * water * nitro]
    return jnp.stack(columns, axis=1)


def edge_weights(padded):
    center = padded[1:-1].astype(jnp.float32)
    north = padded[:-2].astype(jnp.float32)
    south = padded[2:].astype(jnp.float32)

    def link(near):
        return jnp.where(near >= 0.0, 0.25 + 0.75 * center * near, 0.0)

    east = jnp.roll(center, -1, axis=1)
    west = jnp.roll(center, 1, axis=1)
    stacked = [link(north), link(south), link(east), link(west), center]
    return [v[:, None, :] for v in stacked]


def apply_operator(field, gram, weights):
    w_north, w_south, w_east, w_west, cropland = weights
    padded_field = padded_2(field, (("cell", 0),), 1)
    north = padded_field[:-2]
    south = padded_field[2:]
    lapl = w_north * (field - north) + w_south * (field - south)
    lapl = (
        lapl
        + w_east * (field - jnp.roll(field, -1, axis=2))
        + w_west * (field - jnp.roll(field, 1, axis=2))
    )
    data = cropland * jnp.einsum("kj,rjw->rkw", gram, field, precision=lax.Precision.HIGHEST)
    return data + lambda_smooth * lapl + ridge_term * field


def squares(residual):
    return lax.psum(jnp.sum(residual * residual), "cell")


def body(scen_inputs, yields, crop_mask):
    tile_rows = crop_mask.shape[0]
    row_width = crop_mask.shape[1]
    n_terms = 34
    total_scen = scen_inputs.shape[0] * lax.axis_size("cell")
    scale = 1.0 / (total_scen * yields.shape[1])
    design = design_terms(scen_inputs)
    gram = lax.psum(jnp.dot(design.T, design, precision=lax.Precision.HIGHEST) / total_scen, "cell")
    repeated = jnp.repeat(design.astype(jnp.bfloat16), yields.shape[1], axis=0)
    sample_rows = repeated.shape[0]
    flat = yields.reshape(sample_rows, lax.axis_size("cell") * tile_rows * row_width)
    prod = lax.dot_general(
        repeated, flat, (((0,), (0,)), ((), ())), preferred_element_type=jnp.float32
    )
    rhs = (
        lax.psum_scatter(
            jnp.transpose(
                prod.reshape(n_terms, lax.axis_size("cell") * tile_rows, row_width), (1, 0, 2)
            ),
            "cell",
            scatter_dimension=0,
            tiled=True,
        )
        * scale
    )
    padded_mask = padded_2(crop_mask + 1, (("cell", 0),), 1) - 1
    weights = edge_weights(padded_mask)
    coefs = jnp.zeros_like(rhs)
    residual = rhs
    direction = rhs
    norm_now = squares(residual)
    for step in range(ITERS):
        image = apply_operator(direction, gram, weights)
        alpha = norm_now / lax.psum(jnp.sum(direction * image), "cell")
        coefs = coefs + alpha * direction
        residual = residual - alpha * image
        norm_next = squares(residual)
        direction = residual + norm_next / norm_now * direction
        norm_now = norm_next
    return (coefs, residual)


def solution(mesh):
    in_specs = (P("cell", None), P("cell", None, None, "group"), P("cell", "group"))
    out_specs = (P("cell", None, "group"), P("cell", None, "group"))
    return jax.shard_map(body, mesh=mesh, in_specs=in_specs, out_specs=out_specs, check_vma=False)
```

profile of v0, /device:TPU:0, one launch (start us, length us, event | category | flops | bytes accessed | tf_op | source)
XLA Modules:
  0.0 274.8 jit_solution(3711348706236193892)
XLA Ops:
  7.2 0.0 reduce-scatter.2.cloned.1.call-start
  7.2 0.8 copy.16
  8.0 0.0 copy-start.1
  8.0 0.1 slice_multiply_fusion.23
  8.1 0.1 slice_multiply_fusion.4
  8.1 0.1 slice_multiply_fusion.15
  8.2 0.2 stack.3
  8.5 5.5 %fusion.3 = f32[64,34,128]{2,1,0:T(8,128)} fusion(bf16[240,34]{1,0:T(8,128)(2,1)S(1)} %reshape.17, bf16[30,8,64,128]{3,2,1,0:T(8,128)(2,1)} %bitcast.57), kind=kOutput, calls=%fused_computation.4 | convolution fusion | flops 133693440 | bytes 5062592 | tf_op jit(solution)/shard_map/dot_general | solution.py:86
  14.0 0.0 reduce-scatter.2.cloned.1.call-update
  14.0 0.0 copy-done.1
  14.0 2.4 collective-permute-start
  16.4 1.3 collective-permute-start.1
  17.7 0.2 convolution_multiply_fusion.3
  17.9 64.1 %psum.50 = f32[34,34]{1,0:T(8,128)S(1)} all-reduce(f32[34,34]{1,0:T(8,128)S(1)} %convolution_multiply_fusion.3), channel_id=1, replica_groups=mesh['group'=2,'cell'=16] {'cell'}, use_global_device_ids=true, to_apply=%region_3.4 | all-reduce | flops 1156 | bytes 9248 | tf_op jit(solution)/shard_map/psum | solution.py:82
  82.0 0.0 collective-permute-done
  82.0 0.0 collective-permute-done.1
  82.1 0.1 fusion.58
  82.1 0.1 fusion.59
  82.2 0.1 add_select_fusion.3
  82.3 0.0 reduce-scatter.2.cloned.1.call-done
  82.3 0.0 copy-start
  82.3 1.0 broadcast_multiply_fusion
  83.3 0.1 fusion.55
  83.4 1.3 collective-permute-start.2
  84.7 1.3 collective-permute-start.3
  86.0 0.1 fusion.56
  86.0 0.0 collective-permute-done.2
  86.1 1.7 collective-permute-done.3
  87.7 1.7 multiply_reduce_fusion.4
  89.5 30.3 %all-reduce = (f32[]{:T(128)}, f32[]{:T(128)}) all-reduce(f32[]{:T(128)} %get-tuple-element.9, f32[]{:T(128)} %get-tuple-element.8), channel_id=1, replica_groups=mesh['group'=2,'cell'=16] {'cell'}, use_global_device_ids=true, to_apply=%region_2.3 | all-reduce | flops 2 | bytes 16 | tf_op jit(solution)/shard_map/psum | solution.py:72
  121.2 1.5 multiply_reduce_fusion.3
  122.7 30.1 %psum.52 = f32[]{:T(128)} all-reduce(f32[]{:T(128)} %multiply_reduce_fusion.3), channel_id=1, replica_groups=mesh['group'=2,'cell'=16] {'cell'}, use_global_device_ids=true, to_apply=%region_7.8 | all-reduce | flops 1 | bytes 8 | tf_op jit(solution)/shard_map/psum | solution.py:72
  154.1 0.9 multiply_add_fusion.2
  155.1 0.1 fusion.52
  155.2 1.8 collective-permute-start.4
  156.9 1.3 collective-permute-start.5
  158.2 0.1 fusion.53
  158.3 0.0 collective-permute-done.4
  158.3 1.7 collective-permute-done.5
  160.0 0.8 multiply_reduce_fusion.2
  160.9 32.1 %psum.53 = f32[]{:T(128)} all-reduce(f32[]{:T(128)} %get-tuple-element.74), channel_id=1, replica_groups=mesh['group'=2,'cell'=16] {'cell'}, use_global_device_ids=true, to_apply=%region_9.10 | all-reduce | flops 1 | bytes 8 | tf_op jit(solution)/shard_map/psum | solution.py:108
  194.3 1.5 multiply_reduce_fusion.1
  195.8 30.1 %psum.54 = f32[]{:T(128)} all-reduce(f32[]{:T(128)} %get-tuple-element.12), channel_id=1, replica_groups=mesh['group'=2,'cell'=16] {'cell'}, use_global_device_ids=true, to_apply=%region_11.12 | all-reduce | flops 1 | bytes 8 | tf_op jit(solution)/shard_map/psum | solution.py:72
  227.3 0.1 fusion.49
  227.4 1.8 collective-permute-start.6
  229.2 1.3 collective-permute-start.7
  230.5 0.1 fusion.50
  230.6 0.0 collective-permute-done.6
  230.6 1.7 collective-permute-done.7
  232.3 0.8 multiply_reduce_fusion
  233.1 32.1 %psum.55 = f32[]{:T(128)} all-reduce(f32[]{:T(128)} %get-tuple-element.76), channel_id=1, replica_groups=mesh['group'=2,'cell'=16] {'cell'}, use_global_device_ids=true, to_apply=%region_13.14 | all-reduce | flops 1 | bytes 8 | tf_op jit(solution)/shard_map/psum | solution.py:108
  266.6 0.0 copy-done
  266.6 0.7 copy.19
  267.3 0.6 copy.20
  (13 shorter events, 0.1 us)
Async XLA Ops:
  7.2 75.1 %reduce-scatter.2.cloned.1.call-start = ((), (), s32[]{:S(2)}) async-start(), calls=%async_computation.1 | async-start | bytes 1392640 | tf_op jit(solution)/shard_map/reduce_scatter | solution.py:90
  8.0 6.0 %copy-start.1 = (s32[4,128]{1,0:T(4,128)S(1)}, s32[4,128]{1,0:T(4,128)}, u32[]{:S(2)}) copy-start(s32[4,128]{1,0:T(4,128)} %param.5) | copy-start | bytes 6148
  14.0 68.0 %collective-permute-start = (s32[1,128]{1,0:T(1,128)S(1)}, s32[1,128]{1,0:T(1,128)S(1)}, u32[]{:S(2)}, u32[]{:S(2)}) collective-permute-start(s32[1,128]{1,0:T(1,128)S(1)} %get-tuple-element.71), channel_id=1, source_target_pairs={{0,1},{1,2},{2,3},{3,4},{4,5},{5,6},{6,7},{7,8},{8,9},{9,10},{10,1... | collective-permute-start | bytes 1544 | tf_op jit(solution)/shard_map/ppermute | solution.py:18
  16.4 65.6 %collective-permute-start.1 = (s32[1,128]{1,0:T(1,128)S(1)}, s32[1,128]{1,0:T(1,128)S(1)}, u32[]{:S(2)}, u32[]{:S(2)}) collective-permute-start(s32[1,128]{1,0:T(1,128)S(1)} %get-tuple-element.72), channel_id=1, source_target_pairs={{1,0},{2,1},{3,2},{4,3},{5,4},{6,5},{7,6},{8,7},{9,8},{10,9},{11,1... | collective-permute-start | bytes 1544 | tf_op jit(solution)/shard_map/ppermute | solution.py:21
  82.3 184.3 %copy-start = (f32[4,34,128]{2,1,0:T(8,128)S(1)}, f32[4,34,128]{2,1,0:T(8,128)}, u32[]{:S(2)}) copy-start(f32[4,34,128]{2,1,0:T(8,128)} %reduce-scatter.2.cloned.1.call-done) | copy-start | bytes 208900
  83.4 2.7 collective-permute-start.2
  84.7 3.1 %collective-permute-start.3 = (f32[1,34,128]{2,1,0:T(8,128)S(1)}, f32[1,34,128]{2,1,0:T(8,128)S(1)}, u32[]{:S(2)}, u32[]{:S(2)}) collective-permute-start(f32[1,34,128]{2,1,0:T(8,128)S(1)} %get-tuple-element.35), channel_id=1, source_target_pairs={{1,0},{2,1},{3,2},{4,3},{5,4},{6,5},{7,6},{8,7},{9,8},{10,9},{11,1... | collective-permute-start | bytes 52232 | tf_op jit(solution)/shard_map/ppermute | solution.py:21
  155.2 3.2 %collective-permute-start.4 = (f32[1,34,128]{2,1,0:T(8,128)S(1)}, f32[1,34,128]{2,1,0:T(8,128)S(1)}, u32[]{:S(2)}, u32[]{:S(2)}) collective-permute-start(f32[1,34,128]{2,1,0:T(8,128)S(1)} %get-tuple-element.28), channel_id=1, source_target_pairs={{0,1},{1,2},{2,3},{3,4},{4,5},{5,6},{6,7},{7,8},{8,9},{9,10},{10,1... | collective-permute-start | bytes 52232 | tf_op jit(solution)/shard_map/ppermute | solution.py:18
  156.9 3.1 %collective-permute-start.5 = (f32[1,34,128]{2,1,0:T(8,128)S(1)}, f32[1,34,128]{2,1,0:T(8,128)S(1)}, u32[]{:S(2)}, u32[]{:S(2)}) collective-permute-start(f32[1,34,128]{2,1,0:T(8,128)S(1)} %get-tuple-element.29), channel_id=1, source_target_pairs={{1,0},{2,1},{3,2},{4,3},{5,4},{6,5},{7,6},{8,7},{9,8},{10,9},{11,1... | collective-permute-start | bytes 52232 | tf_op jit(solution)/shard_map/ppermute | solution.py:21
  227.4 3.2 %collective-permute-start.6 = (f32[1,34,128]{2,1,0:T(8,128)S(1)}, f32[1,34,128]{2,1,0:T(8,128)S(1)}, u32[]{:S(2)}, u32[]{:S(2)}) collective-permute-start(f32[1,34,128]{2,1,0:T(8,128)S(1)} %get-tuple-element.22), channel_id=1, source_target_pairs={{0,1},{1,2},{2,3},{3,4},{4,5},{5,6},{6,7},{7,8},{8,9},{9,10},{10,1... | collective-permute-start | bytes 52232 | tf_op jit(solution)/shard_map/ppermute | solution.py:18
  229.2 3.1 %collective-permute-start.7 = (f32[1,34,128]{2,1,0:T(8,128)S(1)}, f32[1,34,128]{2,1,0:T(8,128)S(1)}, u32[]{:S(2)}, u32[]{:S(2)}) collective-permute-start(f32[1,34,128]{2,1,0:T(8,128)S(1)} %get-tuple-element.23), channel_id=1, source_target_pairs={{1,0},{2,1},{3,2},{4,3},{5,4},{6,5},{7,6},{8,7},{9,8},{10,9},{11,1... | collective-permute-start | bytes 52232 | tf_op jit(solution)/shard_map/ppermute | solution.py:21
Sparse Core Ops, SparseCore 0:
  14.1 61.1 reduce-scatter.1
where the time goes:
time: 276 us; the launch traced here: 275 us
  blocking collectives  219 us (79%)
  between operations  21 us (8%)
  starting transfers between devices  12.4 us (4%)
  matrix products  9.17 us (3%)
  other arithmetic  5.31 us (2%)
  waiting for transfers between devices  5.09 us (2%)
  local copies, waits for them, and re-layouts  2.94 us (1%)
    psum x3, blocking collectives, squares(): return lax.psum(jnp.sum(residual * residual), 'cell')  90.6 us
    psum x2, blocking collectives, body(): alpha = norm_now / lax.psum(jnp.sum(direction * image), 'cell')  64.3 us
    psum x1, blocking collectives, body(): lax.psum(jnp.dot(design.T, design, precision=lax.Precision.HIGHEST) / tot...  64.1 us
    ppermute x4, starting transfers between devices, padded_2(): lax.ppermute(lax.slice_in_dim(block, block.shape[dim] - width, None, axis...  7.18 us
  transfers between devices with their start and end apart: 9, of which 3 were waited for; matrix products, arithmetic and copies ran while one was open for 0% of the time, Pallas kernels for 0%

commit v1 on v0

v1 whole, which is shorter than its diff:
```python
import functools

import jax
import jax.numpy as jnp
import numpy as np
from jax import lax
from jax.experimental import pallas as pl
from jax.experimental.pallas import tpu as pltpu
from jax.sharding import PartitionSpec as P

ITERS = 3
TERMS = 34
HALF = TERMS // 2
HROWS = HALF * 8
KROWS = TERMS * 8
PACKED = (HALF + 1) // 2
LAMBDA = 0.5
RIDGE = 0.05
MESH = pl.DeviceIdType.MESH
HIGHEST = lax.Precision.HIGHEST
F32 = jnp.float32
BF16 = jnp.bfloat16


def term_factors():
    terms = [(4, 4, 4)] + [(a, 4, 4) for a in range(4)] + [(a, a, 4) for a in range(4)]
    terms += [(i, j, 4) for i in range(4) for j in range(i + 1, 4)]
    terms += [(a, a, a) for a in range(4)]
    terms += [(i, i, j) for i in range(4) for j in range(4) if i != j]
    terms += [(0, 1, 2), (0, 1, 3), (0, 2, 3)]
    chosen = np.zeros((3, 40, 8), np.float32)
    for k, factors in enumerate(terms):
        for place, level in enumerate(factors):
            chosen[place, k, level] = 1.0
    return chosen.reshape(120, 8)


def iota(shape, dim):
    return lax.broadcasted_iota(jnp.int32, shape, dim)


def dot_nt(a, b, precision=None):
    return lax.dot_general(
        a, b, (((1,), (1,)), ((), ())), precision=precision, preferred_element_type=F32
    )


def dot_nn(a, b, precision=None):
    return jnp.dot(a, b, precision=precision, preferred_element_type=F32)


def three_parts(x):
    first = x.astype(BF16)
    rest = x - first.astype(F32)
    second = rest.astype(BF16)
    third = (rest - second.astype(F32)).astype(BF16)
    return first, second, third


def kernel(n, scen_ref, sel_ref, mask_ref, y_ref, coefs_ref, res_ref,
           ybuf, sbuf, part, r1, r2, r3, chip, pack_up, pack_low, halo, mwin, mhalo,
           lvl, mom, lhs_ref,
           ysem, s1s, s1r, s2s, s2r, s3s, s3r, cs, cr, hs, hr, ms, mr, ls, lr, ps, pr):
    nz = n // 4
    me = lax.axis_index("cell")
    core = me % 2
    mine_y = (me // 2) % 2
    mine_z = me // 4
    chip_id = me // 2
    chips = n // 2
    sibling = me + 1 - 2 * core
    across = me + 2 - 4 * mine_y
    scens, years = y_ref.shape[0], y_ref.shape[1]
    total = scens * n

    def zone(i):
        return (mine_z + 1 + i) % nz

    def load(i):
        rows = pl.ds(pl.multiple_of(zone(i) * 16, 16), 16)
        return pltpu.make_async_copy(y_ref.at[:, :, rows, :], ybuf.at[i], ysem.at[i])

    for i in range(nz):
        load(i).start()

    barrier = pltpu.get_barrier_semaphore()

    def greet(o, carry):
        pl.semaphore_signal(barrier, inc=1, device_id={"cell": (me + o) % n}, device_id_type=MESH)
        return carry

    lax.fori_loop(1, n, greet, 0)

    spots = (iota((8, 4), 0) == iota((8, 4), 1)).astype(F32)
    turned = dot_nt(spots, scen_ref[...], HIGHEST)
    own = jnp.concatenate([turned, jnp.zeros((8, 128 - scens), F32)], axis=1)
    own = own + ((iota((8, 128), 0) == 4) & (iota((8, 128), 1) < scens)).astype(F32)
    lvl[me] = own

    def copy(src, dst, send, recv, to):
        return pltpu.make_async_remote_copy(
            src_ref=src, dst_ref=dst, send_sem=send, recv_sem=recv,
            device_id={"cell": to}, device_id_type=MESH,
        )

    mask_down = copy(mask_ref, mhalo.at[0], ms.at[0], mr.at[0], (me + 1) % n)
    mask_up = copy(mask_ref, mhalo.at[1], ms.at[1], mr.at[1], (me + n - 1) % n)

    pl.semaphore_wait(barrier, n - 1)

    def spread(buf, send, recv):
        def go(o, carry):
            copy(buf.at[me], buf.at[me], send.at[o], recv.at[me], (me + o) % n).start()
            return carry

        lax.fori_loop(1, n, go, 0)

    def gather(buf, send, recv):
        def go(o, carry):
            source = (me + o) % n
            copy(buf.at[source], buf.at[source], send.at[o], recv.at[source], source).wait_recv()
            return carry

        lax.fori_loop(1, n, go, 0)

    def drain(buf, send, recv):
        def go(o, carry):
            copy(buf.at[me], buf.at[me], send.at[o], recv.at[me], (me + o) % n).wait_send()
            return carry

        lax.fori_loop(1, n, go, 0)

    spread(lvl, ls, lr)
    mask_down.start()
    mask_up.start()

    def design_of(levels):
        factors = dot_nn(sel_ref[...], levels, HIGHEST)
        return factors[0:40] * factors[40:80] * factors[80:120]

    widen = (iota((KROWS, 40), 0) // 8 == iota((KROWS, 40), 1)).astype(BF16)
    low = design_of(own).astype(BF16)
    tall = dot_nn(widen, low).astype(BF16)
    by_scen = (iota((scens * 8, 128), 0) // 8 == iota((scens * 8, 128), 1)).astype(BF16)
    full = dot_nt(tall, by_scen)
    same_row = iota((KROWS, scens * 8), 0) % 8 == iota((KROWS, scens * 8), 1) % 8
    lhs_ref[...] = jnp.where(same_row, full, 0.0).astype(BF16)

    def stage1(i):
        return copy(part.at[i, 1 - core], r1.at[i], s1s.at[i], s1r.at[i], sibling)

    def stage2(i):
        return copy(part.at[i, core, 1 - mine_y], r2.at[i], s2s.at[i], s2r.at[i], across)

    def stage3(i):
        to = zone(i) * 4 + me % 4
        return copy(part.at[i, core, mine_y], r3.at[mine_z], s3s.at[i], s3r.at[mine_z], to)

    def compute(i):
        load(i).wait()

        def years_of(s, carry):
            added = jnp.sum(ybuf[i, s].astype(F32), axis=0)
            rows = pl.ds(pl.multiple_of(s * 8, 8), 8)
            sbuf[rows, 0:128] = added[0:8]
            sbuf[rows, 128:256] = added[8:16]
            return carry

        lax.fori_loop(0, scens, years_of, 0, unroll=4)
        lhs = lhs_ref[...]
        first, second, third = three_parts(sbuf[...])
        prod = dot_nn(lhs, first) + (dot_nn(lhs, second) + dot_nn(lhs, third))
        for h in range(2):
            for y in range(2):
                part[i, h, y] = prod[h * HROWS:(h + 1) * HROWS, y * 128:(y + 1) * 128]
        stage1(i).start()

    def finish1(i):
        stage1(i).wait_recv()
        part[i, core, 1 - mine_y] = part[i, core, 1 - mine_y] + r1[i, 1 - mine_y]
        stage2(i).start()

    def finish2(i):
        stage2(i).wait_recv()
        added = part[i, core, mine_y] + r1[i, mine_y] + r2[i]
        if i < nz - 1:
            part[i, core, mine_y] = added
            stage3(i).start()
        else:
            r3[mine_z] = added

    for i in range(nz):
        compute(i)
        if i >= 1:
            finish1(i - 1)
        if i >= 2:
            finish2(i - 2)
    finish1(nz - 1)
    if nz >= 2:
        finish2(nz - 2)

    gather(lvl, ls, lr)
    levels = jnp.concatenate([lvl[i] for i in range(n)], axis=1)
    design = design_of(levels)
    gram = dot_nt(design, design, HIGHEST) * (1.0 / total)
    diag_block = iota((KROWS, KROWS), 0) % 8 == iota((KROWS, KROWS), 1) % 8
    gram_parts = []
    for piece in three_parts(gram):
        wide = dot_nt(dot_nn(widen, piece).astype(BF16), widen)
        gram_parts.append(jnp.where(diag_block, wide, 0.0).astype(BF16))
    g1, g2, g3 = gram_parts

    mask_down_in = copy(mhalo.at[0], mhalo.at[0], ms.at[0], mr.at[0], (me + n - 1) % n)
    mask_up_in = copy(mhalo.at[1], mhalo.at[1], ms.at[1], mr.at[1], (me + 1) % n)
    mask_down_in.wait_recv()
    mask_up_in.wait_recv()
    mwin[0:4, :] = jnp.where(me > 0, mhalo[0].astype(F32), -1.0)
    mwin[4:8, :] = mask_ref[...].astype(F32)
    mwin[8:12, :] = jnp.where(me < n - 1, mhalo[1].astype(F32), -1.0)
    mwin[12:16, :] = jnp.full((4, 128), -1.0, F32)
    center_a, center_b = mwin[0:8, :], mwin[8:16, :]
    sub = iota((8, 128), 0)

    def north_south(a, b):
        axis = a.ndim - 2
        here = sub if a.ndim == 2 else sub[None]
        down_a, down_b = pltpu.roll(a, 1, axis), pltpu.roll(b, 1, axis)
        up_a, up_b = pltpu.roll(a, 7, axis), pltpu.roll(b, 7, axis)
        return (down_a, jnp.where(here == 0, down_a, down_b),
                jnp.where(here == 7, up_b, up_a), up_b)

    def sides(a):
        axis = a.ndim - 1
        return pltpu.roll(a, 127, axis), pltpu.roll(a, 1, axis)

    north_a, north_b, south_a, south_b = north_south(center_a, center_b)

    def weights_of(center, north, south):
        def link(near):
            return jnp.where(near >= 0.0, 0.25 + 0.75 * center * near, 0.0) * LAMBDA

        east, west = sides(center)
        links = [link(north), link(south), link(east), link(west)]
        return links + [links[0] + links[1] + links[2] + links[3] + RIDGE, center]

    weights_a = weights_of(center_a, north_a, south_a)
    weights_b = weights_of(center_b, north_b, south_b)

    finish2(nz - 1)
    for j in range(1, nz):
        source = (mine_z + j) % nz
        copy(r3.at[source], r3.at[source], s3s.at[0], s3r.at[source], source * 4 + me % 4).wait_recv()
    summed = r3[0]
    for z in range(1, nz):
        summed = summed + r3[z]
    summed = summed * (1.0 / (total * years))
    chip[core] = summed
    swap = copy(chip.at[core], chip.at[core], cs, cr.at[core], sibling)
    swap.start()
    tiles = summed.reshape(HALF, 8, 128)
    front = tiles[0:PACKED]
    back = jnp.concatenate([tiles[PACKED:HALF], tiles[PACKED - 1:PACKED]], axis=0)
    upper = sub[None] < 4
    pack_up[...] = jnp.where(upper, pltpu.roll(front, 4, 1), back).reshape(PACKED * 8, 128)
    pack_low[...] = jnp.where(upper, front, pltpu.roll(back, 4, 1)).reshape(PACKED * 8, 128)
    send_up = copy(pack_up, halo.at[core], hs.at[0], hr.at[core], ((chip_id + 1) % chips) * 2)
    send_low = copy(pack_low, halo.at[core], hs.at[1], hr.at[core], ((chip_id + chips - 1) % chips) * 2 + 1)
    send_up.start()
    send_low.start()
    copy(chip.at[1 - core], chip.at[1 - core], cs, cr.at[1 - core], sibling).wait_recv()
    near_chip = jnp.where(core == 0, (chip_id + chips - 1) % chips, (chip_id + 1) % chips)
    for h in range(2):
        copy(halo.at[h], halo.at[h], hs.at[0], hr.at[h], near_chip * 2 + h).wait_recv()
    inside = jnp.where(core == 0, chip_id > 0, chip_id < chips - 1)
    edge = []
    for h in range(2):
        got = halo[h].reshape(PACKED, 8, 128)
        edge += [got, pltpu.roll(got[0:HALF - PACKED], 4, 1)]
    edge = jnp.concatenate(edge, axis=0)
    edge = jnp.where(inside, edge, 0.0)
    whole = jnp.concatenate([chip[0], chip[1]], axis=0).reshape(TERMS, 8, 128)
    moved = pltpu.roll(whole, 4, 1)
    first = core == 0
    v0a = jnp.where(first, jnp.where(upper, edge, moved), whole)
    v0b = jnp.where(first, moved, edge)

    def gram_times(field):
        f1, f2, f3 = three_parts(field)
        small = dot_nn(g3, f1) + dot_nn(g1, f3) + dot_nn(g2, f2)
        return dot_nn(g1, f1) + ((dot_nn(g2, f1) + dot_nn(g1, f2)) + small)

    def image_of(tile, north, south, data, weights):
        w_n, w_s, w_e, w_w, w_all, crop = [w[None] for w in weights]
        east, west = sides(tile)
        out = w_all * tile - w_n * north - w_s * south - w_e * east - w_w * west
        return out + crop * data

    def operator(a, b, both):
        n_a, n_b, s_a, s_b = north_south(a, b)
        flat = a.reshape(KROWS, 128)
        if both:
            flat = jnp.concatenate([flat, b.reshape(KROWS, 128)], axis=1)
        data = gram_times(flat)
        out_a = image_of(a, n_a, s_a, data[:, 0:128].reshape(TERMS, 8, 128), weights_a)
        if not both:
            return out_a, None
        return out_a, image_of(b, n_b, s_b, data[:, 128:256].reshape(TERMS, 8, 128), weights_b)

    v1a, v1b = operator(v0a, v0b, True)
    v2a, v2b = operator(v1a, v1b, True)
    v3a, _ = operator(v2a, v2b, False)

    pairs = [(v0a, v0a), (v0a, v1a), (v1a, v1a), (v1a, v2a), (v2a, v2a), (v2a, v3a), (v3a, v3a)]
    packed = jnp.zeros((8, 128), F32)
    for j, (p, q) in enumerate(pairs):
        tile = jnp.sum(p * q, axis=0)
        row = jnp.sum(jnp.where(sub >= 4, tile, 0.0), axis=0, keepdims=True)
        packed = jnp.where(sub == j, row, packed)
    mom[me] = packed
    spread(mom, ps, pr)
    gather(mom, ps, pr)
    sums = mom[0]
    for i in range(1, n):
        sums = sums + mom[i]
    sums = jnp.broadcast_to(jnp.sum(sums, axis=1, keepdims=True), (8, 128))
    m = [sums[j:j + 1, :] for j in range(7)]

    one = jnp.ones((1, 128), F32)
    res, direction, coef = [one], [one], []
    norm = m[0]

    def inner(p, q, shift):
        out = None
        for i, a in enumerate(p):
            for j, b in enumerate(q):
                term = a * b * m[i + j + shift]
                out = term if out is None else out + term
        return out

    def plus(p, q):
        size = max(len(p), len(q))
        out = []
        for i in range(size):
            if i < len(p) and i < len(q):
                out.append(p[i] + q[i])
            else:
                out.append(p[i] if i < len(p) else q[i])
        return out

    for step in range(ITERS):
        alpha = norm / inner(direction, direction, 1)
        coef = plus(coef, [alpha * d for d in direction])
        zero = jnp.zeros((1, 128), F32)
        res = plus(res, [zero] + [-alpha * d for d in direction])
        if step < ITERS - 1:
            fresh = inner(res, res, 0)
            beta = fresh / norm
            direction = plus(res, [beta * d for d in direction])
            norm = fresh

    basis = [v0a, v1a, v2a, v3a]

    def combine(factors):
        out = factors[0][None] * basis[0]
        for f, v in zip(factors[1:], basis[1:]):
            out = out + f[None] * v
        return jnp.swapaxes(out, 0, 1)[4:8]

    coefs_ref[...] = combine(coef)
    res_ref[...] = combine(res)

    drain(lvl, ls, lr)
    drain(mom, ps, pr)
    mask_down.wait_send()
    mask_up.wait_send()
    for i in range(nz):
        stage1(i).wait_send()
        stage2(i).wait_send()
        if i < nz - 1:
            stage3(i).wait_send()
    swap.wait_send()
    send_up.wait_send()
    send_low.wait_send()


def body(n, scen_inputs, yields, crop_mask):
    nz = n // 4
    scens, years = yields.shape[0], yields.shape[1]
    vmem = pl.BlockSpec(memory_space=pltpu.VMEM)
    dma = pltpu.SemaphoreType.DMA
    out = jax.ShapeDtypeStruct((4, TERMS, 128), F32)
    return pl.pallas_call(
        functools.partial(kernel, n),
        out_shape=(out, out),
        in_specs=[vmem, vmem, vmem, pl.BlockSpec(memory_space=pl.ANY)],
        out_specs=(vmem, vmem),
        scratch_shapes=[
            pltpu.VMEM((nz, scens, years, 16, 128), BF16),
            pltpu.VMEM((scens * 8, 256), F32),
            pltpu.VMEM((nz, 2, 2, HROWS, 128), F32),
            pltpu.VMEM((nz, 2, HROWS, 128), F32),
            pltpu.VMEM((nz, HROWS, 128), F32),
            pltpu.VMEM((nz, HROWS, 128), F32),
            pltpu.VMEM((2, HROWS, 128), F32),
            pltpu.VMEM((PACKED * 8, 128), F32),
            pltpu.VMEM((PACKED * 8, 128), F32),
            pltpu.VMEM((2, PACKED * 8, 128), F32),
            pltpu.VMEM((16, 128), F32),
            pltpu.VMEM((2, 4, 128), jnp.int32),
            pltpu.VMEM((n, 8, 128), F32),
            pltpu.VMEM((n, 8, 128), F32),
            pltpu.VMEM((KROWS, scens * 8), BF16),
            dma((nz,)),
            dma((nz,)), dma((nz,)),
            dma((nz,)), dma((nz,)),
            dma((nz,)), dma((nz,)),
            dma, dma((2,)),
            dma((2,)), dma((2,)),
            dma((2,)), dma((2,)),
            dma((n,)), dma((n,)),
            dma((n,)), dma((n,)),
        ],
        compiler_params=pltpu.CompilerParams(
            collective_id=0, has_side_effects=True, vmem_limit_bytes=48 * 1024 * 1024
        ),
    )(scen_inputs, jnp.asarray(term_factors()), crop_mask, yields)


def solution(mesh):
    in_specs = (P("cell", None), P("cell", None, None, "group"), P("cell", "group"))
    out_specs = (P("cell", None, "group"), P("cell", None, "group"))
    return jax.shard_map(
        functools.partial(body, mesh.shape["cell"]),
        mesh=mesh, in_specs=in_specs, out_specs=out_specs, check_vma=False,
    )
```

time: 276 us -> 39.4 us (0.14)
  blocking collectives: 219 us -> 0 us
  Pallas kernels: 0 us -> 32.8 us
  between operations: 21 us -> 0.64 us
  starting transfers between devices: 12.4 us -> 0 us
  matrix products: 9.17 us -> 0 us
  other arithmetic: 5.31 us -> 0 us
  waiting for transfers between devices: 5.09 us -> 0 us
    psum x6 -> x0, blocking collectives: 219 us -> none  [the longest x3 90.6 us: squares(): return lax.psum(jnp.sum(residual * residual), 'cell')]
    pallas_call x0 -> x1, Pallas kernels: none -> 32.8 us  [body(): pl.pallas_call(functools.partial(kernel, n), out_shape=(out, out), in_spe...]
    ppermute x8 -> x0, starting transfers between devices: 12.4 us -> none  [the longest x4 7.18 us: padded_2(): lax.ppermute(lax.slice_in_dim(block, block.shape[dim] - width, None, axis...]
    dot_general x5 -> x0, matrix products: 9.17 us -> none  [the longest x1 5.51 us: body(): lax.dot_general(repeated, flat, (((0,), (0,)), ((), ())), preferred_eleme...]
    ppermute x8 -> x0, waiting for transfers between devices: 5.08 us -> none  [the longest x4 5.06 us: padded_2(): lax.ppermute(lax.slice_in_dim(block, 0, width, axis=dim), axis, backward)]
    reduce_sum x2 -> x0, other arithmetic: 3.04 us -> none  [squares(): return lax.psum(jnp.sum(residual * residual), 'cell')]
  transfers between devices with their start and end apart: 9 -> 0, of which waited for: 3 -> 0; matrix products, arithmetic and copies ran while one was open for 0% -> 0% of each run, Pallas kernels for 0% -> 0%
where the time goes in v1:
time: 39.4 us; the launch traced here: 39.2 us
  Pallas kernels  32.8 us (83%)
  local copies, waits for them, and re-layouts  5.68 us (14%)
  between operations  0.64 us (2%)
    pallas_call x1, Pallas kernels, body(): pl.pallas_call(functools.partial(kernel, n), out_shape=(out, out), in_spe...  32.8 us
    unnamed x7, local copies, waits for them, and re-layouts  4.38 us
    pallas_call x2, local copies, waits for them, and re-layouts, body(): pl.pallas_call(functools.partial(kernel, n), out_shape=(out, out), in_spe...  1.3 us

profile of v1, /device:TPU:0, one launch (start us, length us, event | category | flops | bytes accessed | tf_op | source)
XLA Modules:
  0.0 39.2 jit_solution(2714818152622252022)
XLA Ops:
  0.6 0.8 %copy.6.scen_ref = f32[24,4]{1,0:T(8,128)S(1)} copy(f32[24,4]{0,1:T(4,128)} %param.4) | data formatting | bytes 768 | tf_op args[0]
  1.4 0.0 copy-start
  1.4 2.1 %copy-done = bf16[24,10,64,128]{3,2,1,0:T(8,128)(2,1)S(1)} copy-done((bf16[24,10,64,128]{3,2,1,0:T(8,128)(2,1)S(1)}, bf16[24,10,64,128]{3,2,1,0:T(8,128)(2,1)}, u32[]{:S(2)}) %copy-start) | copy-done | bytes 3932184
  3.5 0.0 copy-start.1
  3.5 0.8 %copy-done.1 = f32[120,8]{1,0:T(8,128)S(1)} copy-done((f32[120,8]{1,0:T(8,128)S(1)}, f32[120,8]{1,0:T(8,128)}, u32[]{:S(2)}) %copy-start.1) | copy-done | bytes 3864
  4.3 0.0 copy-start.2
  4.3 0.7 %copy-done.2 = s32[4,128]{1,0:T(4,128)S(1)} copy-done((s32[4,128]{1,0:T(4,128)S(1)}, s32[4,128]{1,0:T(4,128)}, u32[]{:S(2)}) %copy-start.2) | copy-done | bytes 2072
  5.0 32.8 %shard_map.59 = (f32[4,34,128]{2,1,0:T(8,128)S(1)}, f32[4,34,128]{2,1,0:T(8,128)S(1)}) custom-call(f32[24,4]{1,0:T(8,128)S(1)} %copy.6.scen_ref, f32[120,8]{1,0:T(8,128)S(1)} %copy-done.1, s32[4,128]{1,0:T(4,128)S(1)} %copy-done.2, bf16[24,10,64,128]{3,2,1,0:T(8,128)(2,1)S(1)} %copy-done), custom_call_target="tpu_custom_call" | custom-call | tf_op jit(solution)/shard_map/pallas_call | solution.py:392
  37.9 0.7 %copy.7 = f32[4,34,128]{2,0,1:T(4,128)} copy(f32[4,34,128]{2,1,0:T(8,128)S(1)} %get-tuple-element.2) | data formatting | bytes 139264 | tf_op jit(solution)/shard_map/pallas_call | solution.py:392
  38.5 0.6 %copy.8 = f32[4,34,128]{2,0,1:T(4,128)} copy(f32[4,34,128]{2,1,0:T(8,128)S(1)} %get-tuple-element.3) | data formatting | bytes 139264 | tf_op jit(solution)/shard_map/pallas_call | solution.py:392
Async XLA Ops:
  1.4 2.1 %copy-start = (bf16[24,10,64,128]{3,2,1,0:T(8,128)(2,1)S(1)}, bf16[24,10,64,128]{3,2,1,0:T(8,128)(2,1)}, u32[]{:S(2)}) copy-start(bf16[24,10,64,128]{3,2,1,0:T(8,128)(2,1)} %y_ref.1) | copy-start | bytes 11796484
  3.5 0.8 %copy-start.1 = (f32[120,8]{1,0:T(8,128)S(1)}, f32[120,8]{1,0:T(8,128)}, u32[]{:S(2)}) copy-start(f32[120,8]{1,0:T(8,128)} %constant.2.clone.sel_ref) | copy-start | bytes 11524
  4.3 0.7 %copy-start.2 = (s32[4,128]{1,0:T(4,128)S(1)}, s32[4,128]{1,0:T(4,128)}, u32[]{:S(2)}) copy-start(s32[4,128]{1,0:T(4,128)} %mask_ref.1) | copy-start | bytes 6148

commit v2 on v1

--- a/solution.py
+++ b/solution.py
@@ -8,7 +8,6 @@
 from jax.experimental.pallas import tpu as pltpu
 from jax.sharding import PartitionSpec as P
 
-ITERS = 3
 TERMS = 34
 HALF = TERMS // 2
 HROWS = HALF * 8
@@ -49,18 +48,16 @@
     return jnp.dot(a, b, precision=precision, preferred_element_type=F32)
 
 
-def three_parts(x):
+def two_parts(x):
     first = x.astype(BF16)
-    rest = x - first.astype(F32)
-    second = rest.astype(BF16)
-    third = (rest - second.astype(F32)).astype(BF16)
-    return first, second, third
-
-
-def kernel(n, scen_ref, sel_ref, mask_ref, y_ref, coefs_ref, res_ref,
+    return first, (x - first.astype(F32)).astype(BF16)
+
+
+def kernel(n, scen_hbm, sel_hbm, mask_hbm, y_ref, coefs_ref, res_ref,
+           scen_ref, sel_ref, mask_ref,
            ybuf, sbuf, part, r1, r2, r3, chip, pack_up, pack_low, halo, mwin, mhalo,
-           lvl, mom, lhs_ref,
-           ysem, s1s, s1r, s2s, s2r, s3s, s3r, cs, cr, hs, hr, ms, mr, ls, lr, ps, pr):
+           lvl, mom_a, mom_b, lhs_ref,
+           ins, ysem, s1s, s1r, s2s, s2r, s3s, s3r, cs, cr, hs, hr, ms, mr, ls, lr, pas, par, pbs, pbr):
     nz = n // 4
     me = lax.axis_index("cell")
     core = me % 2
@@ -80,20 +77,28 @@
         rows = pl.ds(pl.multiple_of(zone(i) * 16, 16), 16)
         return pltpu.make_async_copy(y_ref.at[:, :, rows, :], ybuf.at[i], ysem.at[i])
 
+    small = [
+        pltpu.make_async_copy(scen_hbm, scen_ref, ins.at[0]),
+        pltpu.make_async_copy(sel_hbm, sel_ref, ins.at[1]),
+        pltpu.make_async_copy(mask_hbm, mask_ref, ins.at[2]),
+    ]
+    for move in small:
+        move.start()
     for i in range(nz):
         load(i).start()
 
     barrier = pltpu.get_barrier_semaphore()
 
     def greet(o, carry):
-        pl.semaphore_signal(barrier, inc=1, device_id={"cell": (me + o) % n}, device_id_type=MESH)
+        pl.semaphore_signal(barrier, inc=1, device_id={"cell": lax.rem(me + o, n)}, device_id_type=MESH)
         return carry
 
     lax.fori_loop(1, n, greet, 0)
 
-    spots = (iota((8, 4), 0) == iota((8, 4), 1)).astype(F32)
-    turned = dot_nt(spots, scen_ref[...], HIGHEST)
-    own = jnp.concatenate([turned, jnp.zeros((8, 128 - scens), F32)], axis=1)
+    for move in small:
+        move.wait()
+    turned = jnp.concatenate([scen_ref[...], jnp.zeros((4, 128 - scens), F32)], axis=1)
+    own = jnp.concatenate([turned, jnp.zeros((4, 128), F32)], axis=0)
     own = own + ((iota((8, 128), 0) == 4) & (iota((8, 128), 1) < scens)).astype(F32)
     lvl[me] = own
 
@@ -106,33 +111,13 @@
     mask_down = copy(mask_ref, mhalo.at[0], ms.at[0], mr.at[0], (me + 1) % n)
     mask_up = copy(mask_ref, mhalo.at[1], ms.at[1], mr.at[1], (me + n - 1) % n)
 
-    pl.semaphore_wait(barrier, n - 1)
-
     def spread(buf, send, recv):
-        def go(o, carry):
-            copy(buf.at[me], buf.at[me], send.at[o], recv.at[me], (me + o) % n).start()
-            return carry
-
-        lax.fori_loop(1, n, go, 0)
-
-    def gather(buf, send, recv):
-        def go(o, carry):
-            source = (me + o) % n
-            copy(buf.at[source], buf.at[source], send.at[o], recv.at[source], source).wait_recv()
-            return carry
-
-        lax.fori_loop(1, n, go, 0)
-
-    def drain(buf, send, recv):
-        def go(o, carry):
-            copy(buf.at[me], buf.at[me], send.at[o], recv.at[me], (me + o) % n).wait_send()
-            return carry
-
-        lax.fori_loop(1, n, go, 0)
-
-    spread(lvl, ls, lr)
-    mask_down.start()
-    mask_up.start()
+        for o in range(1, n):
+            copy(buf.at[me], buf.at[me], send, recv, lax.rem(me + o, n)).start()
+
+    def all_but_one(buf, send, recv):
+        others = buf.at[pl.ds(0, n - 1)]
+        return copy(others, others, send, recv, sibling)
 
     def design_of(levels):
         factors = dot_nn(sel_ref[...], levels, HIGHEST)
@@ -168,12 +153,18 @@
 
         lax.fori_loop(0, scens, years_of, 0, unroll=4)
         lhs = lhs_ref[...]
-        first, second, third = three_parts(sbuf[...])
-        prod = dot_nn(lhs, first) + (dot_nn(lhs, second) + dot_nn(lhs, third))
+        first, second = two_parts(sbuf[...])
+        prod = dot_nn(lhs, first) + dot_nn(lhs, second)
         for h in range(2):
             for y in range(2):
                 part[i, h, y] = prod[h * HROWS:(h + 1) * HROWS, y * 128:(y + 1) * 128]
+        if i == 0:
+            pl.semaphore_wait(barrier, n - 1)
         stage1(i).start()
+        if i == 0:
+            spread(lvl, ls, lr)
+            mask_down.start()
+            mask_up.start()
 
     def finish1(i):
         stage1(i).wait_recv()
@@ -199,16 +190,16 @@
     if nz >= 2:
         finish2(nz - 2)
 
-    gather(lvl, ls, lr)
+    all_but_one(lvl, ls, lr).wait_recv()
     levels = jnp.concatenate([lvl[i] for i in range(n)], axis=1)
     design = design_of(levels)
     gram = dot_nt(design, design, HIGHEST) * (1.0 / total)
     diag_block = iota((KROWS, KROWS), 0) % 8 == iota((KROWS, KROWS), 1) % 8
     gram_parts = []
-    for piece in three_parts(gram):
+    for piece in two_parts(gram):
         wide = dot_nt(dot_nn(widen, piece).astype(BF16), widen)
         gram_parts.append(jnp.where(diag_block, wide, 0.0).astype(BF16))
-    g1, g2, g3 = gram_parts
+    g1, g2 = gram_parts
 
     mask_down_in = copy(mhalo.at[0], mhalo.at[0], ms.at[0], mr.at[0], (me + n - 1) % n)
     mask_up_in = copy(mhalo.at[1], mhalo.at[1], ms.at[1], mr.at[1], (me + 1) % n)
@@ -285,9 +276,8 @@
     v0b = jnp.where(first, moved, edge)
 
     def gram_times(field):
-        f1, f2, f3 = three_parts(field)
-        small = dot_nn(g3, f1) + dot_nn(g1, f3) + dot_nn(g2, f2)
-        return dot_nn(g1, f1) + ((dot_nn(g2, f1) + dot_nn(g1, f2)) + small)
+        f1, f2 = two_parts(field)
+        return dot_nn(g1, f1) + (dot_nn(g2, f1) + dot_nn(g1, f2))
 
     def image_of(tile, north, south, data, weights):
         w_n, w_s, w_e, w_w, w_all, crop = [w[None] for w in weights]
@@ -306,71 +296,56 @@
             return out_a, None
         return out_a, image_of(b, n_b, s_b, data[:, 128:256].reshape(TERMS, 8, 128), weights_b)
 
+    def pack(pairs):
+        packed = jnp.zeros((8, 128), F32)
+        for j, (p, q) in enumerate(pairs):
+            tile = jnp.sum(p * q, axis=0)
+            row = jnp.sum(jnp.where(sub >= 4, tile, 0.0), axis=0, keepdims=True)
+            packed = jnp.where(sub == j, row, packed)
+        return packed
+
+    def sums_of(buf):
+        sums = buf[0]
+        for i in range(1, n):
+            sums = sums + buf[i]
+        sums = jnp.broadcast_to(jnp.sum(sums, axis=1, keepdims=True), (8, 128))
+        return [sums[j:j + 1, :] for j in range(7)]
+
     v1a, v1b = operator(v0a, v0b, True)
+    mom_a[me] = pack([(v0a, v0a), (v0a, v1a), (v1a, v1a)])
+    spread(mom_a, pas, par)
     v2a, v2b = operator(v1a, v1b, True)
-    v3a, _ = operator(v2a, v2b, False)
-
-    pairs = [(v0a, v0a), (v0a, v1a), (v1a, v1a), (v1a, v2a), (v2a, v2a), (v2a, v3a), (v3a, v3a)]
-    packed = jnp.zeros((8, 128), F32)
-    for j, (p, q) in enumerate(pairs):
-        tile = jnp.sum(p * q, axis=0)
-        row = jnp.sum(jnp.where(sub >= 4, tile, 0.0), axis=0, keepdims=True)
-        packed = jnp.where(sub == j, row, packed)
-    mom[me] = packed
-    spread(mom, ps, pr)
-    gather(mom, ps, pr)
-    sums = mom[0]
-    for i in range(1, n):
-        sums = sums + mom[i]
-    sums = jnp.broadcast_to(jnp.sum(sums, axis=1, keepdims=True), (8, 128))
-    m = [sums[j:j + 1, :] for j in range(7)]
-
-    one = jnp.ones((1, 128), F32)
-    res, direction, coef = [one], [one], []
-    norm = m[0]
-
-    def inner(p, q, shift):
-        out = None
-        for i, a in enumerate(p):
-            for j, b in enumerate(q):
-                term = a * b * m[i + j + shift]
-                out = term if out is None else out + term
-        return out
-
-    def plus(p, q):
-        size = max(len(p), len(q))
-        out = []
-        for i in range(size):
-            if i < len(p) and i < len(q):
-                out.append(p[i] + q[i])
-            else:
-                out.append(p[i] if i < len(p) else q[i])
-        return out
-
-    for step in range(ITERS):
-        alpha = norm / inner(direction, direction, 1)
-        coef = plus(coef, [alpha * d for d in direction])
-        zero = jnp.zeros((1, 128), F32)
-        res = plus(res, [zero] + [-alpha * d for d in direction])
-        if step < ITERS - 1:
-            fresh = inner(res, res, 0)
-            beta = fresh / norm
-            direction = plus(res, [beta * d for d in direction])
-            norm = fresh
-
-    basis = [v0a, v1a, v2a, v3a]
-
-    def combine(factors):
-        out = factors[0][None] * basis[0]
-        for f, v in zip(factors[1:], basis[1:]):
-            out = out + f[None] * v
-        return jnp.swapaxes(out, 0, 1)[4:8]
-
-    coefs_ref[...] = combine(coef)
-    res_ref[...] = combine(res)
-
-    drain(lvl, ls, lr)
-    drain(mom, ps, pr)
+    all_but_one(mom_a, pas, par).wait_recv()
+    m = sums_of(mom_a)
+    alpha0 = m[0] / m[1]
+    beta0 = (m[0] - 2.0 * alpha0 * m[1] + alpha0 * alpha0 * m[2]) / m[0]
+    res1 = v0a - alpha0 * v1a
+    dir1 = res1 + beta0 * v0a
+    image_res1 = v1a - alpha0 * v2a
+    image1a = image_res1 + beta0 * v1a
+    image1b = (v1b - alpha0 * v2b) + beta0 * v1b
+    twice, _ = operator(image1a, image1b, False)
+
+    mom_b[me] = pack([(res1, res1), (dir1, image1a), (res1, image1a), (image1a, image1a),
+                      (res1, image_res1), (image1a, image_res1), (image1a, twice)])
+    spread(mom_b, pbs, pbr)
+    all_but_one(mom_b, pbs, pbr).wait_recv()
+    rr, da, ra, aa, rt, at, aw = sums_of(mom_b)
+    alpha1 = rr / da
+    fresh = rr - 2.0 * alpha1 * ra + alpha1 * alpha1 * aa
+    beta1 = fresh / rr
+    along = (rt + 2.0 * beta1 * ra - 2.0 * alpha1 * at - 2.0 * alpha1 * beta1 * aa
+             + alpha1 * alpha1 * aw + beta1 * beta1 * da)
+    alpha2 = fresh / along
+    res2 = res1 - alpha1 * image1a
+    dir2 = res2 + beta1 * dir1
+    image2 = image_res1 - alpha1 * twice + beta1 * image1a
+    coefs_ref[...] = (alpha0 * v0a + alpha1 * dir1 + alpha2 * dir2)[:, 4:8, :]
+    res_ref[...] = (res2 - alpha2 * image2)[:, 4:8, :]
+
+    all_but_one(lvl, ls, lr).wait_send()
+    all_but_one(mom_a, pas, par).wait_send()
+    all_but_one(mom_b, pbs, pbr).wait_send()
     mask_down.wait_send()
     mask_up.wait_send()
     for i in range(nz):
@@ -387,14 +362,18 @@
     nz = n // 4
     scens, years = yields.shape[0], yields.shape[1]
     vmem = pl.BlockSpec(memory_space=pltpu.VMEM)
+    hbm = pl.BlockSpec(memory_space=pltpu.HBM)
     dma = pltpu.SemaphoreType.DMA
-    out = jax.ShapeDtypeStruct((4, TERMS, 128), F32)
-    return pl.pallas_call(
+    out = jax.ShapeDtypeStruct((TERMS, 4, 128), F32)
+    coefs, residual = pl.pallas_call(
         functools.partial(kernel, n),
         out_shape=(out, out),
-        in_specs=[vmem, vmem, vmem, pl.BlockSpec(memory_space=pl.ANY)],
+        in_specs=[hbm, hbm, hbm, hbm],
         out_specs=(vmem, vmem),
         scratch_shapes=[
+            pltpu.VMEM((4, scens), F32),
+            pltpu.VMEM((120, 8), F32),
+            pltpu.VMEM((4, 128), jnp.int32),
             pltpu.VMEM((nz, scens, years, 16, 128), BF16),
             pltpu.VMEM((scens * 8, 256), F32),
             pltpu.VMEM((nz, 2, 2, HROWS, 128), F32),
@@ -409,21 +388,22 @@
             pltpu.VMEM((2, 4, 128), jnp.int32),
             pltpu.VMEM((n, 8, 128), F32),
             pltpu.VMEM((n, 8, 128), F32),
+            pltpu.VMEM((n, 8, 128), F32),
             pltpu.VMEM((KROWS, scens * 8), BF16),
-            dma((nz,)),
+            dma((3,)), dma((nz,)),
             dma((nz,)), dma((nz,)),
             dma((nz,)), dma((nz,)),
             dma((nz,)), dma((nz,)),
             dma, dma((2,)),
             dma((2,)), dma((2,)),
             dma((2,)), dma((2,)),
-            dma((n,)), dma((n,)),
-            dma((n,)), dma((n,)),
+            dma, dma, dma, dma, dma, dma,
         ],
         compiler_params=pltpu.CompilerParams(
-            collective_id=0, has_side_effects=True, vmem_limit_bytes=48 * 1024 * 1024
+            collective_id=0, has_side_effects=True, vmem_limit_bytes=64512 * 1024
         ),
-    )(scen_inputs, jnp.asarray(term_factors()), crop_mask, yields)
+    )(scen_inputs.T, jnp.asarray(term_factors()), crop_mask, yields)
+    return jnp.transpose(coefs, (1, 0, 2)), jnp.transpose(residual, (1, 0, 2))
 
 
 def solution(mesh):

time: 39.4 us -> 38.8 us (0.985)
  local copies, waits for them, and re-layouts: 5.68 us -> 3.04 us
  Pallas kernels: 32.8 us -> 34.9 us
    pallas_call x1, Pallas kernels: 32.8 us -> 34.9 us  [body(): pl.pallas_call(functools.partial(kernel, n), out_shape=(out, out), in_spe...]
    unnamed x7 -> x2, local copies, waits for them, and re-layouts: 4.38 us -> 3.04 us
    pallas_call x2 -> x0, local copies, waits for them, and re-layouts: 1.3 us -> none  [body(): pl.pallas_call(functools.partial(kernel, n), out_shape=(out, out), in_spe...]
where the time goes in v2:
time: 38.8 us; the launch traced here: 38.6 us
  Pallas kernels  34.9 us (90%)
  local copies, waits for them, and re-layouts  3.04 us (8%)
  between operations  0.64 us (2%)
    pallas_call x1, Pallas kernels, body(): pl.pallas_call(functools.partial(kernel, n), out_shape=(out, out), in_spe...  34.9 us
    unnamed x2, local copies, waits for them, and re-layouts  3.04 us

profile of v2, /device:TPU:0, one launch (start us, length us, event | category | flops | bytes accessed | tf_op | source)
XLA Modules:
  0.0 38.6 jit_solution(10025536354497247301)
XLA Ops:
  0.6 34.9 %shard_map.59 = (f32[34,4,128]{2,1,0:T(4,128)}, f32[34,4,128]{2,1,0:T(4,128)}) custom-call(f32[4,24]{1,0:T(4,128)} %bitcast.5, f32[120,8]{1,0:T(8,128)} %constant.2.clone.sel_hbm, s32[4,128]{1,0:T(4,128)} %mask_hbm.1, bf16[24,10,64,128]{3,2,1,0:T(8,128)(2,1)} %y_ref.1), custom_call_target="tpu_custom_call" | custom-call | tf_op jit(solution)/shard_map/pallas_call | solution.py:368
  35.5 1.5 %copy.8 = f32[4,34,128]{2,0,1:T(4,128)} copy(f32[4,34,128]{2,0,1:T(4,128)} %bitcast.4) | data formatting | bytes 139264
  37.1 1.5 %copy.9 = f32[4,34,128]{2,0,1:T(4,128)} copy(f32[4,34,128]{2,0,1:T(4,128)} %bitcast.3) | data formatting | bytes 139264

commit v3 on v2

--- a/solution.py
+++ b/solution.py
@@ -53,7 +53,7 @@
     return first, (x - first.astype(F32)).astype(BF16)
 
 
-def kernel(n, scen_hbm, sel_hbm, mask_hbm, y_ref, coefs_ref, res_ref,
+def kernel(n, scen_hbm, sel_hbm, mask_hbm, y_ref, out_ref,
            scen_ref, sel_ref, mask_ref,
            ybuf, sbuf, part, r1, r2, r3, chip, pack_up, pack_low, halo, mwin, mhalo,
            lvl, mom_a, mom_b, lhs_ref,
@@ -98,9 +98,9 @@
     for move in small:
         move.wait()
     turned = jnp.concatenate([scen_ref[...], jnp.zeros((4, 128 - scens), F32)], axis=1)
-    own = jnp.concatenate([turned, jnp.zeros((4, 128), F32)], axis=0)
-    own = own + ((iota((8, 128), 0) == 4) & (iota((8, 128), 1) < scens)).astype(F32)
-    lvl[me] = own
+    lvl[me] = turned
+    filled = ((iota((4, 128), 0) == 0) & (iota((4, 128), 1) < scens)).astype(F32)
+    own = jnp.concatenate([turned, filled], axis=0)
 
     def copy(src, dst, send, recv, to):
         return pltpu.make_async_remote_copy(
@@ -192,6 +192,7 @@
 
     all_but_one(lvl, ls, lr).wait_recv()
     levels = jnp.concatenate([lvl[i] for i in range(n)], axis=1)
+    levels = jnp.concatenate([levels, jnp.concatenate([filled] * n, axis=1)], axis=0)
     design = design_of(levels)
     gram = dot_nt(design, design, HIGHEST) * (1.0 / total)
     diag_block = iota((KROWS, KROWS), 0) % 8 == iota((KROWS, KROWS), 1) % 8
@@ -302,12 +303,14 @@
             tile = jnp.sum(p * q, axis=0)
             row = jnp.sum(jnp.where(sub >= 4, tile, 0.0), axis=0, keepdims=True)
             packed = jnp.where(sub == j, row, packed)
-        return packed
+        packed = jnp.sum(packed, axis=1, keepdims=True)
+        return jnp.sum(jnp.where(sub == iota((8, 128), 1), packed, 0.0), axis=0, keepdims=True)
 
     def sums_of(buf):
         sums = buf[0]
         for i in range(1, n):
             sums = sums + buf[i]
+        sums = jnp.where(sub == iota((8, 128), 1), sums, 0.0)
         sums = jnp.broadcast_to(jnp.sum(sums, axis=1, keepdims=True), (8, 128))
         return [sums[j:j + 1, :] for j in range(7)]
 
@@ -340,8 +343,8 @@
     res2 = res1 - alpha1 * image1a
     dir2 = res2 + beta1 * dir1
     image2 = image_res1 - alpha1 * twice + beta1 * image1a
-    coefs_ref[...] = (alpha0 * v0a + alpha1 * dir1 + alpha2 * dir2)[:, 4:8, :]
-    res_ref[...] = (res2 - alpha2 * image2)[:, 4:8, :]
+    solved = alpha0 * v0a + alpha1 * dir1 + alpha2 * dir2
+    out_ref[...] = jnp.where(upper, pltpu.roll(solved, 4, 1), res2 - alpha2 * image2)
 
     all_but_one(lvl, ls, lr).wait_send()
     all_but_one(mom_a, pas, par).wait_send()
@@ -364,12 +367,11 @@
     vmem = pl.BlockSpec(memory_space=pltpu.VMEM)
     hbm = pl.BlockSpec(memory_space=pltpu.HBM)
     dma = pltpu.SemaphoreType.DMA
-    out = jax.ShapeDtypeStruct((TERMS, 4, 128), F32)
-    coefs, residual = pl.pallas_call(
+    both = pl.pallas_call(
         functools.partial(kernel, n),
-        out_shape=(out, out),
+        out_shape=jax.ShapeDtypeStruct((TERMS, 8, 128), F32),
         in_specs=[hbm, hbm, hbm, hbm],
-        out_specs=(vmem, vmem),
+        out_specs=vmem,
         scratch_shapes=[
             pltpu.VMEM((4, scens), F32),
             pltpu.VMEM((120, 8), F32),
@@ -386,9 +388,9 @@
             pltpu.VMEM((2, PACKED * 8, 128), F32),
             pltpu.VMEM((16, 128), F32),
             pltpu.VMEM((2, 4, 128), jnp.int32),
-            pltpu.VMEM((n, 8, 128), F32),
-            pltpu.VMEM((n, 8, 128), F32),
-            pltpu.VMEM((n, 8, 128), F32),
+            pltpu.VMEM((n, 4, 128), F32),
+            pltpu.VMEM((n, 1, 128), F32),
+            pltpu.VMEM((n, 1, 128), F32),
             pltpu.VMEM((KROWS, scens * 8), BF16),
             dma((3,)), dma((nz,)),
             dma((nz,)), dma((nz,)),
@@ -403,7 +405,8 @@
             collective_id=0, has_side_effects=True, vmem_limit_bytes=64512 * 1024
         ),
     )(scen_inputs.T, jnp.asarray(term_factors()), crop_mask, yields)
-    return jnp.transpose(coefs, (1, 0, 2)), jnp.transpose(residual, (1, 0, 2))
+    both = jnp.transpose(both, (1, 0, 2))
+    return both[0:4], both[4:8]
 
 
 def solution(mesh):

time: 38.8 us -> 36.8 us (0.948)
  local copies, waits for them, and re-layouts: 3.04 us -> 1.66 us
  Pallas kernels: 34.9 us -> 34.4 us
    unnamed x2 -> x0, local copies, waits for them, and re-layouts: 3.04 us -> none
    slice x0 -> x1, local copies, waits for them, and re-layouts: none -> 1.66 us  [body(): return (both[0:4], both[4:8])]
    pallas_call x1, Pallas kernels: 34.9 us -> 34.4 us  [body(): pl.pallas_call(functools.partial(kernel, n), out_shape=jax.ShapeDtypeStru...]
where the time goes in v3:
time: 36.8 us; the launch traced here: 36.7 us
  Pallas kernels  34.4 us (93%)
  local copies, waits for them, and re-layouts  1.66 us (5%)
  between operations  0.64 us (2%)
    pallas_call x1, Pallas kernels, body(): pl.pallas_call(functools.partial(kernel, n), out_shape=jax.ShapeDtypeStru...  34.4 us
    slice x1, local copies, waits for them, and re-layouts, body(): return (both[0:4], both[4:8])  1.66 us

profile of v3, /device:TPU:0, one launch (start us, length us, event | category | flops | bytes accessed | tf_op | source)
XLA Modules:
  0.0 36.7 jit_solution(17106087171086717705)
XLA Ops:
  0.6 34.4 %shard_map.59 = f32[34,8,128]{2,1,0:T(8,128)} custom-call(f32[4,24]{1,0:T(4,128)} %bitcast.3, f32[120,8]{1,0:T(8,128)} %constant.2.clone.sel_hbm, s32[4,128]{1,0:T(4,128)} %mask_hbm.1, bf16[24,10,64,128]{3,2,1,0:T(8,128)(2,1)} %y_ref.1), custom_call_target="tpu_custom_call" | custom-call | tf_op jit(solution)/shard_map/pallas_call | solution.py:370
  35.0 1.7 %fusion = (f32[4,34,128]{2,0,1:T(4,128)}, f32[4,34,128]{2,0,1:T(4,128)}) fusion(f32[8,34,128]{2,0,1:T(8,128)} %bitcast.2), kind=kLoop, calls=%fused_computation | loop fusion | bytes 278528 | tf_op jit(solution)/shard_map/slice | solution.py:409

commit v4 on v3

--- a/solution.py
+++ b/solution.py
@@ -71,7 +71,7 @@
     total = scens * n
 
     def zone(i):
-        return (mine_z + 1 + i) % nz
+        return (mine_z + nz // 2 + i) % nz if i < nz // 2 else (mine_z + 1 + i - nz // 2) % nz if i < nz - 1 else mine_z
 
     def load(i):
         rows = pl.ds(pl.multiple_of(zone(i) * 16, 16), 16)
@@ -186,9 +186,9 @@
             finish1(i - 1)
         if i >= 2:
             finish2(i - 2)
-    finish1(nz - 1)
     if nz >= 2:
         finish2(nz - 2)
+    finish1(nz - 1)
 
     all_but_one(lvl, ls, lr).wait_recv()
     levels = jnp.concatenate([lvl[i] for i in range(n)], axis=1)
@@ -246,9 +246,6 @@
     for z in range(1, nz):
         summed = summed + r3[z]
     summed = summed * (1.0 / (total * years))
-    chip[core] = summed
-    swap = copy(chip.at[core], chip.at[core], cs, cr.at[core], sibling)
-    swap.start()
     tiles = summed.reshape(HALF, 8, 128)
     front = tiles[0:PACKED]
     back = jnp.concatenate([tiles[PACKED:HALF], tiles[PACKED - 1:PACKED]], axis=0)
@@ -259,6 +256,9 @@
     send_low = copy(pack_low, halo.at[core], hs.at[1], hr.at[core], ((chip_id + chips - 1) % chips) * 2 + 1)
     send_up.start()
     send_low.start()
+    chip[core] = summed
+    swap = copy(chip.at[core], chip.at[core], cs, cr.at[core], sibling)
+    swap.start()
     copy(chip.at[1 - core], chip.at[1 - core], cs, cr.at[1 - core], sibling).wait_recv()
     near_chip = jnp.where(core == 0, (chip_id + chips - 1) % chips, (chip_id + 1) % chips)
     for h in range(2):

time: 36.8 us -> 36.3 us (0.986)
  Pallas kernels: 34.4 us -> 33.9 us
    pallas_call x1, Pallas kernels: 34.4 us -> 33.9 us  [body(): pl.pallas_call(functools.partial(kernel, n), out_shape=jax.ShapeDtypeStru...]
where the time goes in v4:
time: 36.3 us; the launch traced here: 36.2 us
  Pallas kernels  33.9 us (93%)
  local copies, waits for them, and re-layouts  1.66 us (5%)
  between operations  0.64 us (2%)
    pallas_call x1, Pallas kernels, body(): pl.pallas_call(functools.partial(kernel, n), out_shape=jax.ShapeDtypeStru...  33.9 us
    slice x1, local copies, waits for them, and re-layouts, body(): return (both[0:4], both[4:8])  1.66 us

profile of v4, /device:TPU:0, one launch (start us, length us, event | category | flops | bytes accessed | tf_op | source)
XLA Modules:
  0.0 36.2 jit_solution(13221498042748717370)
XLA Ops:
  0.6 33.9 %shard_map.59 = f32[34,8,128]{2,1,0:T(8,128)} custom-call(f32[4,24]{1,0:T(4,128)} %bitcast.3, f32[120,8]{1,0:T(8,128)} %constant.2.clone.sel_hbm, s32[4,128]{1,0:T(4,128)} %mask_hbm.1, bf16[24,10,64,128]{3,2,1,0:T(8,128)(2,1)} %y_ref.1), custom_call_target="tpu_custom_call" | custom-call | tf_op jit(solution)/shard_map/pallas_call | solution.py:370
  34.5 1.7 %fusion = (f32[4,34,128]{2,0,1:T(4,128)}, f32[4,34,128]{2,0,1:T(4,128)}) fusion(f32[8,34,128]{2,0,1:T(8,128)} %bitcast.2), kind=kLoop, calls=%fused_computation | loop fusion | bytes 278528 | tf_op jit(solution)/shard_map/slice | solution.py:409
